TPU v7x, 32 devices: a whole 2x2x4 slice. The times are simulated.
32 devices in a mesh: groups: 2 (over y), ctx: 4 (over x, core), head: 4 (over z).
Axes of the slice: x: 2, y: 2, z: 4, core: 2. Of those that a mesh axis runs over, the one named last changes fastest.
Arguments:
- tokens_in: bfloat16 [8192, 4096], P(('groups', 'ctx')), parts along dimension 0, may hold values from -16 to 16
- tempo_ids: int32 [8192], P(('groups', 'ctx')), parts along dimension 0, may hold values from 0 to 63
- tempo_table: bfloat16 [64, 4096], replicated, may hold values from -6 to 6
- w_query: bfloat16 [4096, 2048], P('ctx', 'head'), may hold values from -0.1875 to 0.1875
- w_key: bfloat16 [4096, 2048], P('ctx', 'head'), may hold values from -0.09375 to 0.09375
- w_value: bfloat16 [4096, 2048], P('ctx', 'head'), may hold values from -0.09375 to 0.09375
Outputs:
- attended: bfloat16 [8192, 2048], P(('groups', 'ctx'), 'head'), parts along dimension 0
There are 2 independent parts, one for each index of `groups`. A program takes and returns all parts, laid end to end along the dimension named above; an argument that names none is the same for every part. Nothing has to cross between parts.
All inputs are finite; a program needn't handle non-finite values.
Results may differ from a plain program's by a relative error of at most 0.029.
Values may be sent and summed in bfloat16 or wider, within the bound.
No kernel may reach another device: no remote copies, remote signals or barrier semaphores. Data moves between devices by JAX's collectives and lax.ppermute only.
A program may use at most 64 MiB of HBM per device.

v0:
```python
import jax
import jax.numpy as jnp
from jax import lax
from jax.sharding import PartitionSpec as P

HEAD_DIM = 128
SPAN = 1024
BEACONS = 32
POOL = 32
LOWEST = -1e30


def by_heads(matrix, heads_local):
    return matrix.reshape(matrix.shape[0], heads_local, -1).transpose(1, 0, 2)


def partial_attend(queries, keys, values, allowed):
    scores = jnp.einsum(
        "hqd,hkd->hqk", queries, keys, preferred_element_type=jnp.float32
    ) * queries.shape[-1] ** (-0.5)
    masked = jnp.where(allowed, scores, LOWEST)
    highest = jnp.max(masked, axis=2)
    weights = jnp.where(allowed, jnp.exp(masked - highest[..., None]), 0.0)
    totals = jnp.sum(weights, axis=2)
    summed = jnp.einsum(
        "hqk,hkd->hqd", weights.astype(jnp.bfloat16), values, preferred_element_type=jnp.float32
    )
    return (highest, totals, summed)


def combine_partials(first, second):
    highest = jnp.maximum(first[0], second[0])
    left_factor = jnp.exp(first[0] - highest)
    right_factor = jnp.exp(second[0] - highest)
    totals = first[1] * left_factor + second[1] * right_factor
    summed = first[2] * left_factor[..., None] + second[2] * right_factor[..., None]
    return (highest, totals, summed)


def beacon_partial(
    queries, query_span, beacon_keys, beacon_values, low_rank, high_rank, group, slots_dev
):
    heads_local, query_count, head_size = queries.shape
    block_width = group * slots_dev
    start_state = (
        jnp.full((heads_local, query_count), LOWEST, jnp.float32),
        jnp.zeros((heads_local, query_count), jnp.float32),
        jnp.zeros((heads_local, query_count, head_size), jnp.float32),
    )

    def visit(block, state):
        first_slot = block * block_width
        block_keys = lax.dynamic_slice_in_dim(beacon_keys, first_slot, block_width, 1)
        block_values = lax.dynamic_slice_in_dim(beacon_values, first_slot, block_width, 1)
        slot_index = first_slot + jnp.arange(block_width, dtype=jnp.int32)
        owner = slot_index // slots_dev
        in_range = (owner >= low_rank) & (owner < high_rank)
        earlier = (slot_index // BEACONS)[None, :] < query_span[:, None]
        allowed = (in_range[None, :] & earlier)[None]
        return combine_partials(state, partial_attend(queries, block_keys, block_values, allowed))

    first_block = low_rank // group
    last_block = (high_rank + group - 1) // group
    return lax.fori_loop(first_block, last_block, visit, start_state)


def on_device(tokens_in, tempo_ids, tempo_table, w_query, w_key, w_value):
    row_count = tokens_in.shape[0]
    col_width = w_query.shape[1]
    heads_local = col_width // HEAD_DIM
    ctx_count = lax.axis_size("ctx")
    ctx_rank = lax.axis_index("ctx")
    spans_dev = row_count // SPAN
    slots_dev = spans_dev * BEACONS
    target = max(1, 256 // slots_dev)
    group = min(ctx_count, 1 << target.bit_length() - 1)
    selector = (
        tempo_ids[:, None] == jnp.arange(tempo_table.shape[0], dtype=jnp.int32)[None, :]
    ).astype(jnp.bfloat16)
    hidden = (
        tokens_in.astype(jnp.float32)
        + jnp.dot(selector, tempo_table, preferred_element_type=jnp.float32)
    ).astype(jnp.bfloat16)
    pieces = (
        lax.all_gather(w_query, "ctx", axis=0, tiled=True),
        lax.all_gather(w_key, "ctx", axis=0, tiled=True),
        lax.all_gather(w_value, "ctx", axis=0, tiled=True),
    )
    projected = tuple(
        (jnp.dot(hidden, piece, preferred_element_type=jnp.float32) for piece in pieces)
    )
    queries = projected[0].astype(jnp.bfloat16)
    keys = projected[1].astype(jnp.bfloat16)
    values = projected[2].astype(jnp.bfloat16)
    pool_scale = POOL ** (-0.5)
    own_keys = (
        jnp.sum(keys.reshape(slots_dev, POOL, col_width).astype(jnp.float32), axis=1) * pool_scale
    ).astype(jnp.bfloat16)
    own_values = (
        jnp.sum(values.reshape(slots_dev, POOL, col_width).astype(jnp.float32), axis=1) * pool_scale
    ).astype(jnp.bfloat16)
    every_keys, every_values = (
        lax.all_gather(own_keys, "ctx", axis=0, tiled=True),
        lax.all_gather(own_values, "ctx", axis=0, tiled=True),
    )
    beacon_keys = by_heads(every_keys, heads_local)
    beacon_values = by_heads(every_values, heads_local)
    query_heads = by_heads(queries, heads_local)
    local_span = jnp.arange(row_count, dtype=jnp.int32) // SPAN
    own_span = ctx_rank * spans_dev + local_span

    def fold_spans(matrix):
        return by_heads(matrix, heads_local)

    causal = (
        jnp.arange(SPAN, dtype=jnp.int32)[:, None] >= jnp.arange(SPAN, dtype=jnp.int32)[None, :]
    )[None]
    inside = partial_attend(fold_spans(queries), fold_spans(keys), fold_spans(values), causal)
    inside = (inside[0], inside[1], inside[2])
    upper_rank = ctx_rank + 1
    remote = beacon_partial(
        query_heads,
        own_span,
        beacon_keys,
        beacon_values,
        jnp.zeros((), jnp.int32),
        upper_rank,
        group,
        slots_dev,
    )
    highest, totals, summed = combine_partials(inside, remote)
    attended = summed / totals[..., None]
    return attended.transpose(1, 0, 2).reshape(row_count, col_width).astype(jnp.bfloat16)


def solution(mesh):
    in_specs = (
        P(("groups", "ctx"), None),
        P(("groups", "ctx")),
        P(),
        P("ctx", "head"),
        P("ctx", "head"),
        P("ctx", "head"),
    )
    out_specs = P(("groups", "ctx"), "head")
    return jax.shard_map(
        on_device, mesh=mesh, in_specs=in_specs, out_specs=out_specs, check_vma=False
    )
```

profile of v0, /device:TPU:0, one launch (start us, length us, event | category | flops | bytes accessed | tf_op | source)
XLA Modules:
  0.0 165.5 jit_solution(11830383064842661481)
XLA Ops:
  6.5 0.7 all-gather.4.cloned.1.call-update
  7.3 0.7 all-gather.6.cloned.1.call-update
  8.1 0.7 all-gather.8.cloned.1.call-update
  8.8 1.3 iota_compare_fusion
  10.0 6.9 %add_convert_fusion = bf16[1024,4096]{1,0:T(8,128)(2,1)} fusion(bf16[1024,4096]{1,0:T(8,128)(2,1)} %param.8, bf16[64,4096]{1,0:T(8,128)(2,1)S(1)} %copy-done, s32[1024]{0:T(1024)S(1)} %copy-done.3), kind=kOutput, calls=%fused_computation.34 | convolution fusion | flops 549519360 | bytes 17305600 | tf_op jit(solution)/shard_map/dot_general | solution.py:82
  16.9 29.2 %all-gather.4.cloned.1.call-done = bf16[4096,512]{1,0:T(8,128)(2,1)} async-done(((bf16[1024,512]{1,0:T(8,128)(2,1)}), bf16[4096,512]{1,0:T(8,128)(2,1)}) %all-gather.4.cloned.1.call-update) | async-done | bytes 4194320 | tf_op jit(solution)/shard_map/all_gather | solution.py:85
  46.1 9.1 %convolution_convert_fusion.2 = bf16[1024,512]{0,1:T(8,128)(2,1)S(1)} fusion(bf16[1024,4096]{1,0:T(8,128)(2,1)} %add_convert_fusion, bf16[4096,512]{1,0:T(8,128)(2,1)} %all-gather.4.cloned.1.call-done), kind=kOutput, calls=%fused_computation.46 | convolution fusion | flops 4295491584 | bytes 13631488 | tf_op jit(solution)/shard_map/dot_general | solution.py:90
  55.2 1.3 copy.24
  56.5 25.6 %all-gather.6.cloned.1.call-done = bf16[4096,512]{1,0:T(8,128)(2,1)} async-done(((bf16[1024,512]{1,0:T(8,128)(2,1)}), bf16[4096,512]{1,0:T(8,128)(2,1)}) %all-gather.6.cloned.1.call-update) | async-done | bytes 4194320 | tf_op jit(solution)/shard_map/all_gather | solution.py:86
  82.2 10.0 %convert_reduce_fusion.1 = (f32[32,512]{1,0:T(8,128)S(1)}, bf16[1024,512]{1,0:T(8,128)(2,1)}) fusion(bf16[1024,4096]{1,0:T(8,128)(2,1)} %add_convert_fusion, bf16[4096,512]{1,0:T(8,128)(2,1)} %all-gather.6.cloned.1.call-done), kind=kOutput, calls=%fused_computation.42 | convolution fusion | flops 4296523776 | bytes 13697024 | tf_op jit(solution)/shard_map/dot_general | solution.py:90
  92.2 6.4 %all_gather.18 = bf16[128,512]{1,0:T(8,128)(2,1)S(1)} all-gather(bf16[32,512]{1,0:T(8,128)(2,1)S(1)} %multiply_convert_fusion.1), channel_id=1, replica_groups=mesh['groups'=2,'ctx'=4,'head'=4] {'ctx'}, dimensions={0}, use_global_device_ids=true | all-gather | bytes 163840 | tf_op jit(solution)/shard_map/all_gather | solution.py:103
  98.9 20.0 %all-gather.8.cloned.1.call-done = bf16[4096,512]{1,0:T(8,128)(2,1)} async-done(((bf16[1024,512]{1,0:T(8,128)(2,1)}), bf16[4096,512]{1,0:T(8,128)(2,1)}) %all-gather.8.cloned.1.call-update) | async-done | bytes 4194320 | tf_op jit(solution)/shard_map/all_gather | solution.py:87
  118.9 10.1 %convert_reduce_fusion = (f32[32,512]{1,0:T(8,128)S(1)}, bf16[1024,512]{1,0:T(8,128)(2,1)}) fusion(bf16[1024,4096]{1,0:T(8,128)(2,1)} %add_convert_fusion, bf16[4096,512]{1,0:T(8,128)(2,1)} %all-gather.8.cloned.1.call-done), kind=kOutput, calls=%fused_computation.41 | convolution fusion | flops 4296523776 | bytes 13697024 | tf_op jit(solution)/shard_map/dot_general | solution.py:90
  129.0 5.4 %all_gather.19 = bf16[128,512]{1,0:T(8,128)(2,1)S(1)} all-gather(bf16[32,512]{1,0:T(8,128)(2,1)S(1)} %multiply_convert_fusion), channel_id=1, replica_groups=mesh['groups'=2,'ctx'=4,'head'=4] {'ctx'}, dimensions={0}, use_global_device_ids=true | all-gather | bytes 163840 | tf_op jit(solution)/shard_map/all_gather | solution.py:104
  134.9 5.2 %while.17 = (s32[]{:T(128)}, f32[4,1024]{1,0:T(4,128)S(1)}, f32[4,1024]{1,0:T(4,128)S(1)}, f32[4,1024,128]{2,1,0:T(8,128)S(1)}, s32[]{:T(128)}, /*index=5*/s32[]...) while((s32[]{:T(128)}, f32[4,1024]{1,0:T(4,128)S(1)}, ...), condition=%wide.region_6.7_spmd.clone, body=%wide.region_3.6_spmd.clone.sunk | while | flops 277116288 | bytes 12559769 | solution.py:64
  135.1 1.8 %fusion.61 = (f32[4,1024]{1,0:T(4,128)S(1)}, f32[4,1024,128]{1,2,0:T(8,128)S(1)}) fusion(pred[1024,128]{0,1:T(8,128)(4,1)S(1)} %compare_and_fusion.5, bf16[4,1024,128]{2,1,0:T(8,128)(2,1)} %get-tuple-element.322, bf16[4,128,128]{2,1,0:T(8,128)(2,1)S(1)} %get-tuple-element.323), kind=kOutput, calls=%fused_computation.4.clone.1 | convolution fusion | flops 135786496 | bytes 3424256 | tf_op jit(solution)/shard_map/while/body/hqd,hkd->hqk/dot_general | solution.py:18
  136.9 0.6 fusion.62
  137.5 2.5 %multiply_add_fusion.6 = f32[4,1024,128]{2,1,0:T(8,128)S(1)} fusion(f32[4,1024,128]{2,1,0:T(8,128)S(1)} %get-tuple-element.307, bf16[4,128,128]{2,1,0:T(8,128)(2,1)S(1)} %get-tuple-element.324, f32[4,1024,128]{1,2,0:T(8,128)S(1)} %get-tuple-element.286, f32[4,1024]{1,0:T(4,128)S(1)} %get-tuple-element.290, f32[4,1024]{1,0:T(4,128)S(1)} %get-tuple-element.291, ...), kind=kOutput, calls=%fused_computation.1.clone.1 | convolution fusion | flops 138412032 | bytes 6602752 | tf_op jit(solution)/shard_map/while/body/hqk,hkd->hqd/dot_general | solution.py:25
  140.0 1.9 %copy.32 = f32[4,1024,128]{1,2,0:T(8,128)} copy(f32[4,1024,128]{2,1,0:T(8,128)S(1)} %get-tuple-element.137) | data formatting | bytes 4194304 | tf_op jit(solution)/shard_map/while | solution.py:64
  141.9 1.5 copy.36
  143.4 5.0 %fusion.18 = (f32[4,1024]{1,0:T(4,128)S(1)}, f32[4,1024,1024]{1,2,0:T(8,128)S(1)}) fusion(pred[1024,1024]{0,1:T(8,128)(4,1)} %iota_compare_fusion, bf16[1024,4,128]{2,0,1:T(8,128)(2,1)} %bitcast.56, bf16[1024,512]{1,0:T(8,128)(2,1)} %get-tuple-element.213), kind=kOutput, calls=%fused_computation.35 | convolution fusion | flops 1086320640 | bytes 19939328 | tf_op jit(solution)/shard_map/hqd,hkd->hqk/dot_general | solution.py:18
  148.4 4.2 %fusion.19 = f32[4,1024]{1,0:T(4,128)S(1)} fusion(f32[4,1024,1024]{1,2,0:T(8,128)S(1)} %get-tuple-element.217, f32[4,1024]{1,0:T(4,128)S(1)} %get-tuple-element.216, pred[1024,1024]{0,1:T(8,128)(4,1)S(1)} %copy-done.1), kind=kLoop, calls=%fused_computation.36 | loop fusion | flops 20967424 | bytes 17858560 | tf_op jit(solution)/shard_map/reduce_sum | solution.py:24
  152.6 5.1 %divide_convert_fusion = bf16[4,1024,128]{1,2,0:T(8,128)(2,1)S(1)} fusion(f32[4,1024,128]{1,2,0:T(8,128)S(1)} %copy-done.2, bf16[4,1024,128]{1,2,0:T(8,128)(2,1)S(1)} %bitcast.57, f32[4,1024,1024]{1,2,0:T(8,128)S(1)} %get-tuple-element.217, f32[4,1024]{1,0:T(4,128)S(1)} %get-tuple-element.216, pred[1024,1024]{0,1:T(8,128)(4,1)S(1)} %copy-done.1, ...), kind=kOutput, calls=%fused_computation.43 | convolution fusion | flops 1097334784 | bytes 22085632 | tf_op jit(solution)/shard_map/hqk,hkd->hqd/dot_general | solution.py:25
  157.7 1.3 copy.33
  (26 shorter events, 1.0 us)
Async XLA Ops:
  6.5 3.5 %copy-start = (bf16[64,4096]{1,0:T(8,128)(2,1)S(1)}, bf16[64,4096]{1,0:T(8,128)(2,1)}, u32[]{:S(2)}) copy-start(bf16[64,4096]{1,0:T(8,128)(2,1)} %param.10) | copy-start | bytes 1572868
  6.5 3.5 %copy-start.3 = (s32[1024]{0:T(1024)S(1)}, s32[1024]{0:T(1024)}, u32[]{:S(2)}) copy-start(s32[1024]{0:T(1024)} %param.9) | copy-start | bytes 12292
  6.5 39.6 %all-gather.4.cloned.1.call-start = ((), (), s32[]{:S(2)}) async-start(), calls=%async_computation | async-start | bytes 5242880 | tf_op jit(solution)/shard_map/all_gather | solution.py:85
  7.3 74.9 %all-gather.6.cloned.1.call-start = ((), (), s32[]{:S(2)}) async-start(), calls=%async_computation.1 | async-start | bytes 5242880 | tf_op jit(solution)/shard_map/all_gather | solution.py:86
  8.0 110.9 %all-gather.8.cloned.1.call-start = ((), (), s32[]{:S(2)}) async-start(), calls=%async_computation.2 | async-start | bytes 5242880 | tf_op jit(solution)/shard_map/all_gather | solution.py:87
  143.4 5.0 %copy-start.1 = (pred[1024,1024]{0,1:T(8,128)(4,1)S(1)}, pred[1024,1024]{0,1:T(8,128)(4,1)}, u32[]{:S(2)}) copy-start(pred[1024,1024]{0,1:T(8,128)(4,1)} %iota_compare_fusion) | copy-start | bytes 3145732
  148.4 4.2 %copy-start.2 = (f32[4,1024,128]{1,2,0:T(8,128)S(1)}, f32[4,1024,128]{1,2,0:T(8,128)}, u32[]{:S(2)}) copy-start(f32[4,1024,128]{1,2,0:T(8,128)} %copy.32) | copy-start | bytes 6291460
Sparse Core Ops, SparseCore 0:
  8.9 37.1 all-gather.3
  47.7 34.4 all-gather.5
  83.7 35.1 all-gather.7
where the time goes:
time: 166 us
  waiting for transfers between devices  76.9 us (46%)
  matrix products  50.5 us (30%)
  between operations  13.3 us (8%)
  blocking collectives  11.8 us (7%)
  local copies, waits for them, and re-layouts  6.65 us (4%)
  other arithmetic  6.29 us (4%)
    dot_general x3, matrix products, on_device(): jnp.dot(hidden, piece, preferred_element_type=jnp.float32)  29.2 us
    all_gather x1, waiting for transfers between devices, on_device(): lax.all_gather(w_query, 'ctx', axis=0, tiled=True)  29.2 us
    all_gather x1, waiting for transfers between devices, on_device(): lax.all_gather(w_key, 'ctx', axis=0, tiled=True)  25.6 us
    all_gather x1, waiting for transfers between devices, on_device(): lax.all_gather(w_value, 'ctx', axis=0, tiled=True)  20 us
    dot_general x2, matrix products, partial_attend(): jnp.einsum('hqk,hkd->hqd', weights.astype(jnp.bfloat16), values, preferre...  7.61 us
    dot_general x1, matrix products, on_device(): jnp.dot(selector, tempo_table, preferred_element_type=jnp.float32)  6.89 us
    dot_general x2, matrix products, partial_attend(): jnp.einsum('hqd,hkd->hqk', queries, keys, preferred_element_type=jnp.floa...  6.75 us
    all_gather x1, blocking collectives, on_device(): lax.all_gather(own_keys, 'ctx', axis=0, tiled=True)  6.43 us
  transfers between devices with their start and end apart: 3, of which 3 were waited for; matrix products, arithmetic and copies ran while one was open for 17% of the time, Pallas kernels for 0%

commit v1 on v0

--- a/solution.py
+++ b/solution.py
@@ -8,6 +8,34 @@
 BEACONS = 32
 POOL = 32
 LOWEST = -1e30
+
+
+def fields_see(field_in, dim_no=0):
+    block_now, frame_out, placed = (
+        lax.psum(1, "ctx"),
+        lax.axis_index("ctx"),
+        field_in.shape[dim_no],
+    )
+    store = tuple(((k, (k + 1) % block_now) for k in range(block_now)))
+    r1 = jnp.zeros(
+        (*field_in.shape[:dim_no], block_now * placed, *field_in.shape[dim_no + 1 :]),
+        field_in.dtype,
+    )
+    r1 = lax.dynamic_update_slice_in_dim(r1, field_in, frame_out * placed, axis=dim_no)
+    odd = high = field_in
+    long_array = block_now // 2
+    column = tuple(((k, (k - 1) % block_now) for k in range(block_now)))
+    for i0 in [*range(1, long_array + 1)]:
+        odd = lax.ppermute(odd, axis_name="ctx", perm=store)
+        r1 = lax.dynamic_update_slice_in_dim(
+            r1, odd, (frame_out - i0) % block_now * placed, axis=dim_no
+        )
+        if i0 < block_now - long_array:
+            high = lax.ppermute(high, "ctx", column)
+            r1 = lax.dynamic_update_slice_in_dim(
+                r1, high, (frame_out + i0) % block_now * placed, axis=dim_no
+            )
+    return r1
 
 
 def by_heads(matrix, heads_local):
@@ -83,7 +111,7 @@
     ).astype(jnp.bfloat16)
     pieces = (
         lax.all_gather(w_query, "ctx", axis=0, tiled=True),
-        lax.all_gather(w_key, "ctx", axis=0, tiled=True),
+        fields_see(w_key),
         lax.all_gather(w_value, "ctx", axis=0, tiled=True),
     )
     projected = tuple(

time: 166 us -> 147 us (0.89)
  waiting for transfers between devices: 76.9 us -> 53 us
  starting transfers between devices: 0.08 us -> 9.64 us
  matrix products: 50.5 us -> 42.5 us
  local copies, waits for them, and re-layouts: 6.65 us -> 9.53 us
    ppermute x0 -> x3, waiting for transfers between devices: none -> 41.5 us  [the longest x2 41.5 us: fields_see(): odd = lax.ppermute(odd, axis_name='ctx', perm=store)]
    all_gather x1, waiting for transfers between devices: 29.2 us -> 0.02 us  [on_device(): lax.all_gather(w_query, 'ctx', axis=0, tiled=True)]
    all_gather x1 -> x0, waiting for transfers between devices: 25.6 us -> none  [on_device(): lax.all_gather(w_key, 'ctx', axis=0, tiled=True)]
    all_gather x1, waiting for transfers between devices: 20 us -> 10.1 us  [on_device(): lax.all_gather(w_value, 'ctx', axis=0, tiled=True)]
    ppermute x0 -> x3, starting transfers between devices: none -> 9.6 us  [the longest x2 7.62 us: fields_see(): odd = lax.ppermute(odd, axis_name='ctx', perm=store)]
    dot_general x3, matrix products: 29.2 us -> 24.7 us  [on_device(): jnp.dot(hidden, piece, preferred_element_type=jnp.float32)]
    dynamic_update_slice x0 -> x4, local copies, waits for them, and re-layouts: none -> 2.45 us  [the longest x1 2.13 us: fields_see(): lax.dynamic_update_slice_in_dim(r1, high, (frame_out + i0) % block_now *...]
    dot_general x1, matrix products: 6.89 us -> 4.98 us  [on_device(): jnp.dot(selector, tempo_table, preferred_element_type=jnp.float32)]
  transfers between devices with their start and end apart: 3 -> 5, of which waited for: 3 -> 3; matrix products, arithmetic and copies ran while one was open for 17% -> 17% of each run, Pallas kernels for 0% -> 0%
where the time goes in v1:
time: 147 us
  waiting for transfers between devices  53 us (36%)
  matrix products  42.5 us (29%)
  between operations  13.6 us (9%)
  blocking collectives  12.3 us (8%)
  starting transfers between devices  9.64 us (7%)
  local copies, waits for them, and re-layouts  9.53 us (6%)
  other arithmetic  6.29 us (4%)
    ppermute x2, waiting for transfers between devices, fields_see(): odd = lax.ppermute(odd, axis_name='ctx', perm=store)  41.5 us
    dot_general x3, matrix products, on_device(): jnp.dot(hidden, piece, preferred_element_type=jnp.float32)  24.7 us
    all_gather x1, waiting for transfers between devices, on_device(): lax.all_gather(w_value, 'ctx', axis=0, tiled=True)  10.1 us
    ppermute x2, starting transfers between devices, fields_see(): odd = lax.ppermute(odd, axis_name='ctx', perm=store)  7.62 us
    dot_general x2, matrix products, partial_attend(): jnp.einsum('hqk,hkd->hqd', weights.astype(jnp.bfloat16), values, preferre...  7.61 us
    all_gather x1, blocking collectives, on_device(): lax.all_gather(own_keys, 'ctx', axis=0, tiled=True)  6.92 us
    all_gather x1, blocking collectives, on_device(): lax.all_gather(own_values, 'ctx', axis=0, tiled=True)  5.42 us
    dot_general x2, matrix products, partial_attend(): jnp.einsum('hqd,hkd->hqk', queries, keys, preferred_element_type=jnp.floa...  5.18 us
  transfers between devices with their start and end apart: 5, of which 3 were waited for; matrix products, arithmetic and copies ran while one was open for 17% of the time, Pallas kernels for 0%

profile of v1, /device:TPU:0, one launch (start us, length us, event | category | flops | bytes accessed | tf_op | source)
XLA Modules:
  0.0 147.2 jit_solution(5153105360735531426)
XLA Ops:
  6.5 0.7 all-gather.3.cloned.1.call-update
  7.3 0.7 all-gather.5.cloned.1.call-update
  8.6 2.0 %collective-permute-start.1 = (bf16[1024,512]{1,0:T(8,128)(2,1)}, bf16[1024,512]{1,0:T(8,128)(2,1)}, u32[]{:S(2)}, u32[]{:S(2)}) collective-permute-start(bf16[1024,512]{1,0:T(8,128)(2,1)} %param.12), channel_id=1, source_target_pairs={{0,12},{4,0},{8,4},{12,8},{1,13},{5,1},{9,5},{13,9},{2,14},{6,2},{... | collective-permute-start | bytes 3145736 | tf_op jit(solution)/shard_map/ppermute | solution.py:34
  10.5 1.3 iota_compare_fusion
  11.8 29.7 %collective-permute-done = bf16[1024,512]{1,0:T(8,128)(2,1)S(1)} collective-permute-done((bf16[1024,512]{1,0:T(8,128)(2,1)}, bf16[1024,512]{1,0:T(8,128)(2,1)S(1)}, u32[]{:S(2)}, u32[]{:S(2)}) %collective-permute-start) | collective-permute-done | bytes 1048608 | tf_op jit(solution)/shard_map/ppermute | solution.py:29
  41.5 7.1 %collective-permute-start.2 = (bf16[1024,512]{1,0:T(8,128)(2,1)S(1)}, bf16[1024,512]{1,0:T(8,128)(2,1)S(1)}, u32[]{:S(2)}, u32[]{:S(2)}) collective-permute-start(bf16[1024,512]{1,0:T(8,128)(2,1)S(1)} %collective-permute-done), channel_id=1, source_target_pairs={{0,4},{4,8},{8,12},{12,0},{1,5},{5,9},{9,13},{13,1},{2,6},{6,10},{... | collective-permute-start | bytes 3145736 | tf_op jit(solution)/shard_map/ppermute | solution.py:29
  49.0 5.0 %add_convert_fusion = bf16[1024,4096]{1,0:T(8,128)(2,1)S(1)} fusion(bf16[1024,4096]{1,0:T(8,128)(2,1)} %param.8, bf16[64,4096]{1,0:T(8,128)(2,1)S(1)} %copy-done, s32[1024]{0:T(1024)S(1)} %copy-done.7), kind=kOutput, calls=%fused_computation.34 | convolution fusion | flops 549519360 | bytes 17305600 | tf_op jit(solution)/shard_map/dot_general | solution.py:110
  54.1 2.1 %constant_dynamic-update-slice_fusion.1 = bf16[4096,512]{1,0:T(8,128)(2,1)S(1)} fusion(bf16[4096,512]{1,0:T(8,128)(2,1)S(1)} %constant_dynamic-update-slice_fusion.2, bf16[1024,512]{1,0:T(8,128)(2,1)} %collective-permute-done.1, s32[]{:T(128)S(6)} %select_n.82), kind=kLoop, calls=%fused_computation.60 | loop fusion | bytes 2097156 | tf_op jit(solution)/shard_map/dynamic_update_slice | solution.py:35
  56.3 11.8 %collective-permute-done.2 = bf16[1024,512]{1,0:T(8,128)(2,1)S(1)} collective-permute-done((bf16[1024,512]{1,0:T(8,128)(2,1)S(1)}, bf16[1024,512]{1,0:T(8,128)(2,1)S(1)}, u32[]{:S(2)}, u32[]{:S(2)}) %collective-permute-start.2) | collective-permute-done | bytes 1048608 | tf_op jit(solution)/shard_map/ppermute | solution.py:29
  68.2 5.5 %convert_reduce_fusion.1 = (f32[32,512]{1,0:T(8,128)S(1)}, bf16[1024,512]{1,0:T(8,128)(2,1)}) fusion(bf16[1024,4096]{1,0:T(8,128)(2,1)S(1)} %add_convert_fusion, bf16[4096,512]{1,0:T(8,128)(2,1)S(1)} %constant_dynamic-update-slice_fusion), kind=kOutput, calls=%fused_computation.42 | convolution fusion | flops 4296523776 | bytes 13697024 | tf_op jit(solution)/shard_map/dot_general | solution.py:118
  73.7 6.9 %all_gather.14 = bf16[128,512]{1,0:T(8,128)(2,1)S(1)} all-gather(bf16[32,512]{1,0:T(8,128)(2,1)S(1)} %multiply_convert_fusion.1), channel_id=1, replica_groups=mesh['groups'=2,'ctx'=4,'head'=4] {'ctx'}, dimensions={0}, use_global_device_ids=true | all-gather | bytes 163840 | tf_op jit(solution)/shard_map/all_gather | solution.py:131
  80.9 9.1 %convolution_convert_fusion.2 = bf16[1024,512]{0,1:T(8,128)(2,1)S(1)} fusion(bf16[1024,4096]{1,0:T(8,128)(2,1)} %copy-done.2, bf16[4096,512]{1,0:T(8,128)(2,1)} %all-gather.3.cloned.1.call-done), kind=kOutput, calls=%fused_computation.46 | convolution fusion | flops 4295491584 | bytes 13631488 | tf_op jit(solution)/shard_map/dot_general | solution.py:118
  90.1 0.7 copy.24
  90.7 10.1 %all-gather.5.cloned.1.call-done = bf16[4096,512]{1,0:T(8,128)(2,1)} async-done(((bf16[1024,512]{1,0:T(8,128)(2,1)}), bf16[4096,512]{1,0:T(8,128)(2,1)}) %all-gather.5.cloned.1.call-update) | async-done | bytes 4194320 | tf_op jit(solution)/shard_map/all_gather | solution.py:115
  100.8 10.1 %convert_reduce_fusion = (f32[32,512]{1,0:T(8,128)S(1)}, bf16[1024,512]{1,0:T(8,128)(2,1)}) fusion(bf16[1024,4096]{1,0:T(8,128)(2,1)} %copy-done.2, bf16[4096,512]{1,0:T(8,128)(2,1)} %all-gather.5.cloned.1.call-done), kind=kOutput, calls=%fused_computation.41 | convolution fusion | flops 4296523776 | bytes 13697024 | tf_op jit(solution)/shard_map/dot_general | solution.py:118
  110.9 5.4 %all_gather.15 = bf16[128,512]{1,0:T(8,128)(2,1)S(1)} all-gather(bf16[32,512]{1,0:T(8,128)(2,1)S(1)} %multiply_convert_fusion), channel_id=1, replica_groups=mesh['groups'=2,'ctx'=4,'head'=4] {'ctx'}, dimensions={0}, use_global_device_ids=true | all-gather | bytes 163840 | tf_op jit(solution)/shard_map/all_gather | solution.py:132
  116.8 4.1 %while.17 = (s32[]{:T(128)}, f32[4,1024]{1,0:T(4,128)S(1)}, f32[4,1024]{1,0:T(4,128)S(1)}, f32[4,1024,128]{2,1,0:T(8,128)S(1)}, s32[]{:T(128)}, /*index=5*/s32[]...) while((s32[]{:T(128)}, f32[4,1024]{1,0:T(4,128)S(1)}, ...), condition=%wide.region_6.7_spmd.clone, body=%wide.region_3.6_spmd.clone.sunk | while | flops 277116288 | bytes 12559769 | solution.py:92
  118.1 2.5 %multiply_add_fusion.6 = f32[4,1024,128]{2,1,0:T(8,128)S(1)} fusion(f32[4,1024,128]{2,1,0:T(8,128)S(1)} %get-tuple-element.307, bf16[4,128,128]{2,1,0:T(8,128)(2,1)S(1)} %get-tuple-element.324, f32[4,1024,128]{1,2,0:T(8,128)S(1)} %get-tuple-element.286, f32[4,1024]{1,0:T(4,128)S(1)} %get-tuple-element.290, f32[4,1024]{1,0:T(4,128)S(1)} %get-tuple-element.291, ...), kind=kOutput, calls=%fused_computation.1.clone.1 | convolution fusion | flops 138412032 | bytes 6602752 | tf_op jit(solution)/shard_map/while/body/hqk,hkd->hqd/dot_general | solution.py:53
  120.9 1.9 %copy.32 = f32[4,1024,128]{1,2,0:T(8,128)} copy(f32[4,1024,128]{2,1,0:T(8,128)S(1)} %get-tuple-element.137) | data formatting | bytes 4194304 | tf_op jit(solution)/shard_map/while | solution.py:92
  122.8 2.2 %copy.36 = bf16[1024,512]{0,1:T(8,128)(2,1)} copy(bf16[1024,512]{1,0:T(8,128)(2,1)} %get-tuple-element.215) | data formatting | bytes 2097152 | tf_op jit(solution)/shard_map/reshape | solution.py:42
  125.0 4.6 %fusion.18 = (f32[4,1024]{1,0:T(4,128)S(1)}, f32[4,1024,1024]{1,2,0:T(8,128)S(1)}) fusion(pred[1024,1024]{0,1:T(8,128)(4,1)} %iota_compare_fusion, bf16[1024,4,128]{2,0,1:T(8,128)(2,1)S(1)} %bitcast.56, bf16[1024,512]{1,0:T(8,128)(2,1)} %get-tuple-element.213), kind=kOutput, calls=%fused_computation.35 | convolution fusion | flops 1086320640 | bytes 19939328 | tf_op jit(solution)/shard_map/hqd,hkd->hqk/dot_general | solution.py:46
  129.7 4.2 %fusion.19 = f32[4,1024]{1,0:T(4,128)S(1)} fusion(f32[4,1024,1024]{1,2,0:T(8,128)S(1)} %get-tuple-element.217, f32[4,1024]{1,0:T(4,128)S(1)} %get-tuple-element.216, pred[1024,1024]{0,1:T(8,128)(4,1)S(1)} %copy-done.3), kind=kLoop, calls=%fused_computation.36 | loop fusion | flops 20967424 | bytes 17858560 | tf_op jit(solution)/shard_map/reduce_sum | solution.py:52
  134.0 5.1 %divide_convert_fusion = bf16[4,1024,128]{1,2,0:T(8,128)(2,1)S(1)} fusion(f32[4,1024,128]{1,2,0:T(8,128)S(1)} %copy-done.4, bf16[4,1024,128]{1,2,0:T(8,128)(2,1)S(1)} %bitcast.57, f32[4,1024,1024]{1,2,0:T(8,128)S(1)} %get-tuple-element.217, f32[4,1024]{1,0:T(4,128)S(1)} %get-tuple-element.216, pred[1024,1024]{0,1:T(8,128)(4,1)S(1)} %copy-done.3, ...), kind=kOutput, calls=%fused_computation.43 | convolution fusion | flops 1097334784 | bytes 22085632 | tf_op jit(solution)/shard_map/hqk,hkd->hqd/dot_general | solution.py:53
  139.0 1.3 copy.33
  (42 shorter events, 3.2 us)
Async XLA Ops:
  6.5 42.5 %copy-start = (bf16[64,4096]{1,0:T(8,128)(2,1)S(1)}, bf16[64,4096]{1,0:T(8,128)(2,1)}, u32[]{:S(2)}) copy-start(bf16[64,4096]{1,0:T(8,128)(2,1)} %param.10) | copy-start | bytes 1572868
  6.5 42.4 %copy-start.5 = (bf16[1024,512]{1,0:T(8,128)(2,1)S(1)}, bf16[1024,512]{1,0:T(8,128)(2,1)}, u32[]{:S(2)}) copy-start(bf16[1024,512]{1,0:T(8,128)(2,1)} %param.12) | copy-start | bytes 3145732
  6.5 74.4 %all-gather.3.cloned.1.call-start = ((), (), s32[]{:S(2)}) async-start(), calls=%async_computation | async-start | bytes 5242880 | tf_op jit(solution)/shard_map/all_gather | solution.py:113
  7.3 41.8 %copy-start.7 = (s32[1024]{0:T(1024)S(1)}, s32[1024]{0:T(1024)}, u32[]{:S(2)}) copy-start(s32[1024]{0:T(1024)} %param.9) | copy-start | bytes 12292
  7.3 93.5 %all-gather.5.cloned.1.call-start = ((), (), s32[]{:S(2)}) async-start(), calls=%async_computation.1 | async-start | bytes 5242880 | tf_op jit(solution)/shard_map/all_gather | solution.py:115
  8.0 33.5 %collective-permute-start = (bf16[1024,512]{1,0:T(8,128)(2,1)}, bf16[1024,512]{1,0:T(8,128)(2,1)S(1)}, u32[]{:S(2)}, u32[]{:S(2)}) collective-permute-start(bf16[1024,512]{1,0:T(8,128)(2,1)} %param.12), channel_id=1, source_target_pairs={{0,4},{4,8},{8,12},{12,0},{1,5},{5,9},{9,13},{13,1},{2,6},{6,10},{... | collective-permute-start | bytes 3145736 | tf_op jit(solution)/shard_map/ppermute | solution.py:29
  8.6 45.6 %collective-permute-start.1 = (bf16[1024,512]{1,0:T(8,128)(2,1)}, bf16[1024,512]{1,0:T(8,128)(2,1)}, u32[]{:S(2)}, u32[]{:S(2)}) collective-permute-start(bf16[1024,512]{1,0:T(8,128)(2,1)} %param.12), channel_id=1, source_target_pairs={{0,12},{4,0},{8,4},{12,8},{1,13},{5,1},{9,5},{13,9},{2,14},{6,2},{... | collective-permute-start | bytes 3145736 | tf_op jit(solution)/shard_map/ppermute | solution.py:34
  41.5 26.6 %collective-permute-start.2 = (bf16[1024,512]{1,0:T(8,128)(2,1)S(1)}, bf16[1024,512]{1,0:T(8,128)(2,1)S(1)}, u32[]{:S(2)}, u32[]{:S(2)}) collective-permute-start(bf16[1024,512]{1,0:T(8,128)(2,1)S(1)} %collective-permute-done), channel_id=1, source_target_pairs={{0,4},{4,8},{8,12},{12,0},{1,5},{5,9},{9,13},{13,1},{2,6},{6,10},{... | collective-permute-start | bytes 3145736 | tf_op jit(solution)/shard_map/ppermute | solution.py:29
  54.0 19.7 %copy-start.2 = (bf16[1024,4096]{1,0:T(8,128)(2,1)}, bf16[1024,4096]{1,0:T(8,128)(2,1)S(1)}, u32[]{:S(2)}) copy-start(bf16[1024,4096]{1,0:T(8,128)(2,1)S(1)} %add_convert_fusion) | copy-start | bytes 25165828
  125.0 4.6 %copy-start.3 = (pred[1024,1024]{0,1:T(8,128)(4,1)S(1)}, pred[1024,1024]{0,1:T(8,128)(4,1)}, u32[]{:S(2)}) copy-start(pred[1024,1024]{0,1:T(8,128)(4,1)} %iota_compare_fusion) | copy-start | bytes 3145732
  129.7 4.2 %copy-start.4 = (f32[4,1024,128]{1,2,0:T(8,128)S(1)}, f32[4,1024,128]{1,2,0:T(8,128)}, u32[]{:S(2)}) copy-start(f32[4,1024,128]{1,2,0:T(8,128)} %copy.32) | copy-start | bytes 6291460
  129.7 4.2 %copy-start.6 = (bf16[1024,512]{0,1:T(8,128)(2,1)S(1)}, bf16[1024,512]{0,1:T(8,128)(2,1)}, u32[]{:S(2)}) copy-start(bf16[1024,512]{0,1:T(8,128)(2,1)} %copy.36) | copy-start | bytes 3145732
  134.0 6.4 %copy-start.1 = (bf16[64,4096]{1,0:T(8,128)(2,1)S(1)}, bf16[64,4096]{1,0:T(8,128)(2,1)}, u32[]{:S(2)}) copy-start(bf16[64,4096]{1,0:T(8,128)(2,1)} %param.10) | copy-start | bytes 1572868
Sparse Core Ops, SparseCore 0:
  8.9 54.9 all-gather.2
  65.4 35.3 all-gather.4
